TPU v7x, 512 devices: a whole 4x4x16 slice. The times are simulated.
512 devices in a mesh: ctx: 64 (over z, y), vid: 8 (over x, core).
Axes of the slice: x: 4, y: 4, z: 16, core: 2. Of those that a mesh axis runs over, the one named last changes fastest.
Arguments:
- features: bfloat16 [8, 128, 8, 32, 256], P('vid', 'ctx'), may hold values from -6 to 6
- grad_out: bfloat16 [8, 128, 8, 32, 128], P('vid', 'ctx'), may hold values from -6 to 6
- mean_saved: float32 [8, 32], P('vid'), may hold values from -3 to 3
- rstd_saved: float32 [8, 32], P('vid'), may hold values from 0.5 to 2
- latent: float32 [8, 32, 16, 16], P('vid'), may hold values from -6 to 6
- gamma: float32 [256], replicated, may hold values from 0.5 to 1.5
- beta: float32 [256], replicated, may hold values from -3 to 3
- w_scale: float32 [16, 256], replicated, may hold values from -1.5 to 1.5
- b_scale: float32 [256], replicated, may hold values from -3 to 3
- w_shift: float32 [16, 256], replicated, may hold values from -1.5 to 1.5
- b_shift: float32 [256], replicated, may hold values from -3 to 3
- kernel: bfloat16 [6912, 128], replicated, may hold values from -0.078125 to 0.078125
Outputs:
- features_grad: bfloat16 [8, 128, 8, 32, 256], P('vid', 'ctx')
- kernel_grad: float32 [6912, 128], P('ctx', 'vid')
- mod_grads: float32 [2, 16, 256], replicated
- vector_grads: float32 [4, 256], replicated
- latent_grad: float32 [8, 64, 16, 8], P('vid', 'ctx')
All inputs are finite; a program needn't handle non-finite values.
Results may differ from a plain program's by a relative error of at most 0.0029.
Values may be sent and summed in bfloat16 or wider, within the bound.
A program may use at most 64 MiB of HBM per device.

v0:
```python
import jax
import jax.numpy as jnp
from jax import lax
from jax.sharding import PartitionSpec as P

FR_DEV = 2
H = 8
W = 32
C = 256
CO = 128
G = 32
LP = 16
highest = lax.Precision.HIGHEST


def passed_along(value, axis, steps):
    count = lax.axis_size(axis)
    leading, last = (max(0, -steps), min(count, count - steps))
    return lax.ppermute(value, axis, [(source, source + steps) for source in range(leading, last)])


def swapped(value, axis, apart):
    mask = 2**apart
    pairs = [(source, source ^ mask) for source in range(lax.axis_size(axis))]
    return lax.ppermute(value, axis, pairs)


def spread_frame(table):
    grid = table.reshape(H // 4, W // 4, C)
    wide = jnp.broadcast_to(grid[:, None, :, None, :], (H // 4, 4, W // 4, 4, C))
    return wide.reshape(1, H, W, C)


def pool_frames(field):
    frames = field.shape[0]
    return field.reshape(frames, H // 4, 4, W // 4, 4, C).sum(axis=(0, 2, 4)).reshape(LP, C)


def transpose_conv(grad_pad, tap_weights, frames):
    total = jnp.zeros((frames * H * W, C), jnp.float32)
    for frame_tap in range(3):
        for row_tap in range(3):
            for col_tap in range(3):
                source = grad_pad[
                    2 - frame_tap : 2 - frame_tap + frames,
                    2 - row_tap : 2 - row_tap + H,
                    2 - col_tap : 2 - col_tap + W,
                ].reshape(frames * H * W, CO)
                total = total + lax.dot_general(
                    source,
                    tap_weights[frame_tap, row_tap, col_tap],
                    (((1,), (1,)), ((), ())),
                    preferred_element_type=jnp.float32,
                )
    return total.reshape(frames, H, W, C)


def local(
    features,
    grad_out,
    mean_saved,
    rstd_saved,
    latent,
    gamma,
    beta,
    w_scale,
    b_scale,
    w_shift,
    b_shift,
    kernel,
):
    device = lax.axis_index("ctx")
    frames_in = features[0]
    grads_in = grad_out[0]
    mean_chan = jnp.broadcast_to(mean_saved[0][:, None], (G, C // G)).reshape(C)
    rstd_chan = jnp.broadcast_to(rstd_saved[0][:, None], (G, C // G)).reshape(C)
    normed = (frames_in.astype(jnp.float32) - mean_chan) * rstd_chan
    latent_frame = lax.dynamic_index_in_dim(latent[0], device // 2, 0, keepdims=False)
    scale_tab = jnp.einsum("zp,zc->pc", latent_frame, w_scale, precision=highest) + b_scale
    shift_tab = jnp.einsum("zp,zc->pc", latent_frame, w_shift, precision=highest) + b_shift
    scale_map = spread_frame(scale_tab)
    shift_map = spread_frame(shift_tab)
    base_map = normed * gamma + beta
    modulated = base_map * scale_map + shift_map
    squashed = jax.nn.sigmoid(modulated)
    activated = (modulated * squashed).astype(jnp.bfloat16)
    before = passed_along(activated, "ctx", 1)
    leading = jnp.broadcast_to(activated[:1], before.shape)
    before = jnp.where(device == 0, leading, before)
    padded = jnp.pad(jnp.concatenate([before, activated], 0), ((0, 0), (1, 1), (1, 1), (0, 0)))
    tap_weights = kernel.reshape(3, 3, 3, C, CO)
    grads_rows = grads_in.reshape(FR_DEV * H * W, CO)
    pieces = []
    for frame_tap in range(3):
        for row_tap in range(3):
            for col_tap in range(3):
                window = padded[
                    frame_tap : frame_tap + FR_DEV, row_tap : row_tap + H, col_tap : col_tap + W
                ].reshape(FR_DEV * H * W, C)
                pieces.append(
                    lax.dot_general(
                        window,
                        grads_rows,
                        (((0,), (0,)), ((), ())),
                        preferred_element_type=jnp.float32,
                    )
                )
    kernel_term = jnp.stack(pieces).reshape(27 * C, CO)
    beyond = passed_along(grads_in, "ctx", -1)
    grad_pad = jnp.pad(jnp.concatenate([grads_in, beyond], 0), ((2, 0), (1, 1), (1, 1), (0, 0)))
    extended = transpose_conv(grad_pad, tap_weights, FR_DEV + 2)
    act_grad = extended[2:]
    virtual = jnp.where(device == 0, extended[0] + extended[1], 0.0)
    act_grad = act_grad.at[0].add(virtual)
    pre_grad = act_grad * squashed * (1.0 + modulated * (1.0 - squashed))
    features_grad = (pre_grad * scale_map * gamma * rstd_chan).astype(jnp.bfloat16)
    scale_pool = pool_frames(pre_grad * base_map)
    shift_pool = pool_frames(pre_grad)
    mod_part = jnp.stack(
        [
            jnp.einsum("zp,pc->zc", latent_frame, scale_pool, precision=highest),
            jnp.einsum("zp,pc->zc", latent_frame, shift_pool, precision=highest),
        ]
    )
    vec_part = jnp.stack(
        [
            jnp.sum(pre_grad * scale_map * normed, axis=(0, 1, 2)),
            jnp.sum(pre_grad * scale_map, axis=(0, 1, 2)),
            jnp.sum(scale_pool, axis=0),
            jnp.sum(shift_pool, axis=0),
        ]
    )
    latent_sum = jnp.einsum("zc,pc->zp", w_scale, scale_pool, precision=highest) + jnp.einsum(
        "zc,pc->zp", w_shift, shift_pool, precision=highest
    )
    half_len = LP // 2
    parity = device % 2
    own_half = lax.dynamic_slice_in_dim(latent_sum, parity * half_len, half_len, 1)
    far_half = lax.dynamic_slice_in_dim(latent_sum, (1 - parity) * half_len, half_len, 1)
    received = swapped(far_half, "ctx", 0)
    latent_grad = (own_half + received)[None, None]
    mod_grads, vector_grads = lax.psum((mod_part, vec_part), ("ctx", "vid"))
    kernel_part = lax.psum_scatter(kernel_term, "ctx", scatter_dimension=0, tiled=True)
    kernel_grad = lax.psum_scatter(kernel_part, "vid", scatter_dimension=1, tiled=True)
    return (features_grad[None], kernel_grad, mod_grads, vector_grads, latent_grad)


def solution(mesh):
    placed = (
        P("vid", "ctx", None, None, None),
        P("vid", "ctx", None, None, None),
        P("vid", None),
        P("vid", None),
        P("vid", None, None, None),
        P(),
        P(),
        P(),
        P(),
        P(),
        P(),
        P(),
    )
    return jax.shard_map(
        local,
        mesh=mesh,
        in_specs=placed,
        out_specs=(
            P("vid", "ctx", None, None, None),
            P("ctx", "vid"),
            P(),
            P(),
            P("vid", "ctx", None, None),
        ),
        check_vma=False,
    )
```

profile of v0, /device:TPU:8, one launch (start us, length us, event | category | flops | bytes accessed | tf_op | source)
XLA Modules:
  0.0 389.0 jit_solution(9092506910952850593)
XLA Ops:
  7.2 7.7 %collective-permute-start = (bf16[2,8,32,128]{3,2,1,0:T(8,128)(2,1)}, bf16[2,8,32,128]{3,2,1,0:T(8,128)(2,1)S(1)}, u32[]{:S(2)}, u32[]{:S(2)}) collective-permute-start(bf16[2,8,32,128]{3,2,1,0:T(8,128)(2,1)} %bitcast.393), channel_id=1, source_target_pairs={{8,0},{16,8},{24,16},{32,24},{40,32},{48,40},{56,48},{64,56},{72,6... | collective-permute-start | bytes 393224 | tf_op jit(solution)/shard_map/ppermute | solution.py:19
  15.2 0.9 fusion.29
  16.2 0.7 broadcast_in_dim.52
  17.0 0.7 broadcast_in_dim.54
  18.0 0.9 fusion.28
  19.0 0.9 pad_maximum_fusion.1
  20.3 0.9 pad_slice_fusion
  23.2 0.3 convolution_add_fusion.20
  25.3 0.3 convolution_add_fusion.13
  28.9 0.3 convolution_add_fusion.1
  29.9 0.5 fusion.42
  30.3 2.1 collective-permute-start.1
  32.5 6.1 %collective-permute-done.1 = bf16[2,8,32,256]{3,2,1,0:T(8,128)(2,1)S(1)} collective-permute-done((bf16[2,8,32,256]{3,2,1,0:T(8,128)(2,1)S(1)}, bf16[2,8,32,256]{3,2,1,0:T(8,128)(2,1)S(1)}, u32[]{:S(2)}, u32[]{:S(2)}) %collective-permute-start.1) | collective-permute-done | bytes 262176 | tf_op jit(solution)/shard_map/ppermute | solution.py:19
  39.0 0.9 pad_slice_fusion.26
  47.5 1.7 copy-done.2
  49.2 5.2 %copy.25 = f32[6912,128]{0,1:T(8,128)} copy(f32[6912,128]{1,0:T(8,128)} %bitcast.425) | data formatting | bytes 7077888 | tf_op jit(solution)/shard_map/reshape | solution.py:108
  54.5 1.3 dynamic-slice.17
  57.0 1.9 collective-permute-start.2
  59.2 109.6 %all-reduce.3 = (f32[2,16,256]{2,1,0:T(8,128)}, f32[4,256]{1,0:T(4,128)}) all-reduce(f32[2,16,256]{2,1,0:T(8,128)S(1)} %pad_maximum_fusion.2, f32[4,256]{1,0:T(4,128)S(1)} %pad_maximum_fusion.3), channel_id=1, replica_groups=mesh['ctx'=64,'vid'=8] {'ctx','vid'}, use_global_device_ids=true, to_apply=%region_6.7 | all-reduce | flops 9216 | bytes 73728 | tf_op jit(solution)/shard_map/psum | solution.py:142
  168.9 0.8 fusion.38
  169.7 174.6 %all-reduce.6.cloned.1.call-done = f32[6912,128]{0,1:T(8,128)} async-done(((f32[6912,128]{0,1:T(8,128)}), f32[6912,128]{0,1:T(8,128)}) %all-reduce.6.cloned.1.call-update) | async-done | bytes 3538960
  344.3 1.6 constant_dynamic-slice_fusion.1
  345.9 0.6 fusion.55
  346.5 35.6 %reduce-scatter.3.cloned.1.call-done = f32[108,16]{0,1:T(8,128)} async-done(((f32[108,128]{0,1:T(8,128)}), f32[108,16]{0,1:T(8,128)}) %reduce-scatter.3.cloned.1.call-update) | async-done | bytes 6928 | tf_op jit(solution)/shard_map/reduce_scatter | solution.py:144
  (102 shorter events, 17.2 us)
Async XLA Ops:
  7.2 7.8 %copy-start = (f32[1,32,16,16]{1,3,2,0:T(8,128)S(1)}, f32[1,32,16,16]{1,3,2,0:T(8,128)}, u32[]{:S(2)}) copy-start(f32[1,32,16,16]{1,3,2,0:T(8,128)} %param.18) | copy-start | bytes 98308
  7.2 337.1 %all-reduce.6.cloned.1.call-start = ((), (), s32[]{:S(2)}) async-start(), calls=%async_computation.2 | async-start | bytes 7077888
  7.2 11.8 %collective-permute-start = (bf16[2,8,32,128]{3,2,1,0:T(8,128)(2,1)}, bf16[2,8,32,128]{3,2,1,0:T(8,128)(2,1)S(1)}, u32[]{:S(2)}, u32[]{:S(2)}) collective-permute-start(bf16[2,8,32,128]{3,2,1,0:T(8,128)(2,1)} %bitcast.393), channel_id=1, source_target_pairs={{8,0},{16,8},{24,16},{32,24},{40,32},{48,40},{56,48},{64,56},{72,6... | collective-permute-start | bytes 393224 | tf_op jit(solution)/shard_map/ppermute | solution.py:19
  20.0 1.5 copy-start.3
  28.9 1.0 copy-start.4
  28.9 0.9 copy-start.7
  28.9 0.9 copy-start.8
  30.3 8.3 %collective-permute-start.1 = (bf16[2,8,32,256]{3,2,1,0:T(8,128)(2,1)S(1)}, bf16[2,8,32,256]{3,2,1,0:T(8,128)(2,1)S(1)}, u32[]{:S(2)}, u32[]{:S(2)}) collective-permute-start(bf16[2,8,32,256]{3,2,1,0:T(8,128)(2,1)S(1)} %get-tuple-element.26), channel_id=1, source_target_pairs={{0,8},{8,16},{16,24},{24,32},{32,40},{40,48},{48,56},{56,64},{64,7... | collective-permute-start | bytes 786440 | tf_op jit(solution)/shard_map/ppermute | solution.py:19
  38.7 1.2 copy-start.1
  47.4 1.8 copy-start.2
  54.4 2.3 copy-start.6
  54.4 2.5 copy-start.5
  54.4 327.8 %reduce-scatter.3.cloned.1.call-start = ((), (), s32[]{:S(2)}) async-start(), calls=%async_computation.1 | async-start | bytes 73728 | tf_op jit(solution)/shard_map/reduce_scatter | solution.py:144
  57.0 288.9 %collective-permute-start.2 = (f32[16,8]{0,1:T(8,128)S(1)}, f32[16,8]{0,1:T(8,128)S(1)}, u32[]{:S(2)}, u32[]{:S(2)}) collective-permute-start(f32[16,8]{0,1:T(8,128)S(1)} %dynamic-slice_bitcast_fusion), channel_id=1, source_target_pairs={{0,8},{8,0},{16,24},{24,16},{32,40},{40,32},{48,56},{56,48},{64,72... | collective-permute-start | bytes 1544 | tf_op jit(solution)/shard_map/ppermute | solution.py:25
Sparse Core Ops, SparseCore 0:
  54.5 289.7 all-reduce.5
  347.7 34.4 reduce-scatter.2
where the time goes:
time: 390 us; the launch traced here: 389 us
  waiting for transfers between devices  216 us (55%)
  blocking collectives  110 us (28%)
  matrix products  17.6 us (5%)
  between operations  15.5 us (4%)
  local copies, waits for them, and re-layouts  15 us (4%)
  starting transfers between devices  11.8 us (3%)
    unnamed x3, waiting for transfers between devices  175 us
    psum x1, blocking collectives, local(): mod_grads, vector_grads = lax.psum((mod_part, vec_part), ('ctx', 'vid'))  110 us
    reduce_scatter x1, waiting for transfers between devices, local(): lax.psum_scatter(kernel_part, 'vid', scatter_dimension=1, tiled=True)  35.6 us
    ppermute x2, starting transfers between devices, passed_along(): lax.ppermute(value, axis, [(source, source + steps) for source in range(l...  9.81 us
    dot_general x27, matrix products, transpose_conv(): lax.dot_general(source, tap_weights[frame_tap, row_tap, col_tap], (((1,),...  7.88 us
  transfers between devices with their start and end apart: 5, of which 3 were waited for; matrix products, arithmetic and copies ran while one was open for 2% of the time, Pallas kernels for 0%

commit v1 on v0

--- a/solution.py
+++ b/solution.py
@@ -139,7 +139,7 @@
     far_half = lax.dynamic_slice_in_dim(latent_sum, (1 - parity) * half_len, half_len, 1)
     received = swapped(far_half, "ctx", 0)
     latent_grad = (own_half + received)[None, None]
-    mod_grads, vector_grads = lax.psum((mod_part, vec_part), ("ctx", "vid"))
+    mod_grads, vector_grads = lax.psum(lax.psum((mod_part, vec_part), "vid"), "ctx")
     kernel_part = lax.psum_scatter(kernel_term, "ctx", scatter_dimension=0, tiled=True)
     kernel_grad = lax.psum_scatter(kernel_part, "vid", scatter_dimension=1, tiled=True)
     return (features_grad[None], kernel_grad, mod_grads, vector_grads, latent_grad)

time: 390 us -> 410 us (1.051)
  blocking collectives: 110 us -> 304 us
  waiting for transfers between devices: 216 us -> 42.8 us
    psum x1 -> x2, blocking collectives: 110 us -> 304 us  [the longest x1 279 us: local(): lax.psum(lax.psum((mod_part, vec_part), 'vid'), 'ctx')]
    unnamed x3, waiting for transfers between devices: 175 us -> 0.03 us
  transfers between devices with their start and end apart: 5 -> 5, of which waited for: 3 -> 2; matrix products, arithmetic and copies ran while one was open for 2% -> 2% of each run, Pallas kernels for 0% -> 0%
where the time goes in v1:
time: 410 us; the launch traced here: 409 us
  blocking collectives  304 us (74%)
  waiting for transfers between devices  42.8 us (10%)
  matrix products  17.6 us (4%)
  between operations  15.5 us (4%)
  local copies, waits for them, and re-layouts  15 us (4%)
  starting transfers between devices  11.8 us (3%)
    psum x1, blocking collectives, local(): lax.psum(lax.psum((mod_part, vec_part), 'vid'), 'ctx')  279 us
    reduce_scatter x1, waiting for transfers between devices, local(): lax.psum_scatter(kernel_part, 'vid', scatter_dimension=1, tiled=True)  36.6 us
    psum x1, blocking collectives, local(): lax.psum((mod_part, vec_part), 'vid')  24.3 us
    ppermute x2, starting transfers between devices, passed_along(): lax.ppermute(value, axis, [(source, source + steps) for source in range(l...  9.81 us
  transfers between devices with their start and end apart: 5, of which 2 were waited for; matrix products, arithmetic and copies ran while one was open for 2% of the time, Pallas kernels for 0%

profile of v1, /device:TPU:8, one launch (start us, length us, event | category | flops | bytes accessed | tf_op | source)
XLA Modules:
  0.0 409.4 jit_solution(18204605720327332889)
XLA Ops:
  7.2 7.7 %collective-permute-start = (bf16[2,8,32,128]{3,2,1,0:T(8,128)(2,1)}, bf16[2,8,32,128]{3,2,1,0:T(8,128)(2,1)S(1)}, u32[]{:S(2)}, u32[]{:S(2)}) collective-permute-start(bf16[2,8,32,128]{3,2,1,0:T(8,128)(2,1)} %bitcast.393), channel_id=1, source_target_pairs={{8,0},{16,8},{24,16},{32,24},{40,32},{48,40},{56,48},{64,56},{72,6... | collective-permute-start | bytes 393224 | tf_op jit(solution)/shard_map/ppermute | solution.py:19
  15.2 0.9 fusion.29
  16.2 0.7 broadcast_in_dim.52
  17.0 0.7 broadcast_in_dim.54
  18.0 0.9 fusion.28
  19.0 0.9 pad_maximum_fusion.1
  20.3 0.9 pad_slice_fusion
  23.2 0.3 convolution_add_fusion.20
  25.3 0.3 convolution_add_fusion.13
  28.9 0.3 convolution_add_fusion.1
  29.9 0.5 fusion.42
  30.3 2.1 collective-permute-start.1
  32.5 6.1 %collective-permute-done.1 = bf16[2,8,32,256]{3,2,1,0:T(8,128)(2,1)S(1)} collective-permute-done((bf16[2,8,32,256]{3,2,1,0:T(8,128)(2,1)S(1)}, bf16[2,8,32,256]{3,2,1,0:T(8,128)(2,1)S(1)}, u32[]{:S(2)}, u32[]{:S(2)}) %collective-permute-start.1) | collective-permute-done | bytes 262176 | tf_op jit(solution)/shard_map/ppermute | solution.py:19
  39.0 0.9 pad_slice_fusion.26
  47.5 1.7 copy-done.2
  49.2 5.2 %copy.25 = f32[6912,128]{0,1:T(8,128)} copy(f32[6912,128]{1,0:T(8,128)} %bitcast.425) | data formatting | bytes 7077888 | tf_op jit(solution)/shard_map/reshape | solution.py:108
  54.5 1.3 dynamic-slice.17
  57.0 1.9 collective-permute-start.2
  59.2 24.3 %all-reduce.4 = (f32[2,16,256]{2,1,0:T(8,128)S(1)}, f32[4,256]{1,0:T(4,128)S(1)}) all-reduce(f32[2,16,256]{2,1,0:T(8,128)S(1)} %pad_maximum_fusion.2, f32[4,256]{1,0:T(4,128)S(1)} %pad_maximum_fusion.3), channel_id=1, replica_groups=mesh['ctx'=64,'vid'=8] {'vid'}, use_global_device_ids=true, to_apply=%region_6.7 | all-reduce | flops 9216 | bytes 73728 | tf_op jit(solution)/shard_map/psum | solution.py:142
  83.6 279.4 %all-reduce.3 = (f32[2,16,256]{2,1,0:T(8,128)}, f32[4,256]{1,0:T(4,128)}) all-reduce(f32[2,16,256]{2,1,0:T(8,128)S(1)} %get-tuple-element.25, f32[4,256]{1,0:T(4,128)S(1)} %get-tuple-element.26), channel_id=1, replica_groups=mesh['ctx'=64,'vid'=8] {'ctx'}, use_global_device_ids=true, to_apply=%region_7.8 | all-reduce | flops 9216 | bytes 73728 | tf_op jit(solution)/shard_map/psum | solution.py:142
  362.9 0.8 fusion.38
  363.7 1.6 constant_dynamic-slice_fusion.1
  365.3 0.6 fusion.55
  366.0 36.6 %reduce-scatter.3.cloned.1.call-done = f32[108,16]{0,1:T(8,128)} async-done(((f32[108,128]{0,1:T(8,128)}), f32[108,16]{0,1:T(8,128)}) %reduce-scatter.3.cloned.1.call-update) | async-done | bytes 6928 | tf_op jit(solution)/shard_map/reduce_scatter | solution.py:144
  (103 shorter events, 17.2 us)
Async XLA Ops:
  7.2 7.8 %copy-start = (f32[1,32,16,16]{1,3,2,0:T(8,128)S(1)}, f32[1,32,16,16]{1,3,2,0:T(8,128)}, u32[]{:S(2)}) copy-start(f32[1,32,16,16]{1,3,2,0:T(8,128)} %param.18) | copy-start | bytes 98308
  7.2 356.5 %all-reduce.7.cloned.1.call-start = ((), (), s32[]{:S(2)}) async-start(), calls=%async_computation.2 | async-start | bytes 7077888
  7.2 11.8 %collective-permute-start = (bf16[2,8,32,128]{3,2,1,0:T(8,128)(2,1)}, bf16[2,8,32,128]{3,2,1,0:T(8,128)(2,1)S(1)}, u32[]{:S(2)}, u32[]{:S(2)}) collective-permute-start(bf16[2,8,32,128]{3,2,1,0:T(8,128)(2,1)} %bitcast.393), channel_id=1, source_target_pairs={{8,0},{16,8},{24,16},{32,24},{40,32},{48,40},{56,48},{64,56},{72,6... | collective-permute-start | bytes 393224 | tf_op jit(solution)/shard_map/ppermute | solution.py:19
  20.0 1.5 copy-start.3
  28.9 1.0 copy-start.4
  28.9 0.9 copy-start.7
  28.9 0.9 copy-start.8
  30.3 8.3 %collective-permute-start.1 = (bf16[2,8,32,256]{3,2,1,0:T(8,128)(2,1)S(1)}, bf16[2,8,32,256]{3,2,1,0:T(8,128)(2,1)S(1)}, u32[]{:S(2)}, u32[]{:S(2)}) collective-permute-start(bf16[2,8,32,256]{3,2,1,0:T(8,128)(2,1)S(1)} %get-tuple-element.28), channel_id=1, source_target_pairs={{0,8},{8,16},{16,24},{24,32},{32,40},{40,48},{48,56},{56,64},{64,7... | collective-permute-start | bytes 786440 | tf_op jit(solution)/shard_map/ppermute | solution.py:19
  38.7 1.2 copy-start.1
  47.4 1.8 copy-start.2
  54.4 2.3 copy-start.6
  54.4 2.5 copy-start.5
  54.4 348.1 %reduce-scatter.3.cloned.1.call-start = ((), (), s32[]{:S(2)}) async-start(), calls=%async_computation.1 | async-start | bytes 73728 | tf_op jit(solution)/shard_map/reduce_scatter | solution.py:144
  57.0 308.3 %collective-permute-start.2 = (f32[16,8]{0,1:T(8,128)S(1)}, f32[16,8]{0,1:T(8,128)S(1)}, u32[]{:S(2)}, u32[]{:S(2)}) collective-permute-start(f32[16,8]{0,1:T(8,128)S(1)} %dynamic-slice_bitcast_fusion), channel_id=1, source_target_pairs={{0,8},{8,0},{16,24},{24,16},{32,40},{40,32},{48,56},{56,48},{64,72... | collective-permute-start | bytes 1544 | tf_op jit(solution)/shard_map/ppermute | solution.py:25
Sparse Core Ops, SparseCore 0:
  54.5 289.5 all-reduce.6
  365.5 37.0 reduce-scatter.2
